TPU v7x, 32 devices: a whole 2x2x4 slice. The times are simulated.
32 devices in a mesh: region: 4 (over y, x), block: 8 (over z, core).
Axes of the slice: x: 2, y: 2, z: 4, core: 2. Of those that a mesh axis runs over, the one named last changes fastest.
Arguments:
- obs: bfloat16 [512, 32, 128], P(('region', 'block')), may hold values from -6 to 6
- predict: bfloat16 [512, 2, 128, 128], P(('region', 'block')), may hold values from -0.375 to 0.375
- factor: bfloat16 [512, 128, 128], P(('region', 'block')), as said below
- tau: float32 [32], replicated, may hold values from 0.5 to 2
- nbr_dev: int32 [512, 1], P(('region', 'block')), may hold values from 0 to 7; in each aligned block of 16 rows (0 to 15, 16 to 31, ...) at most 4 rows name the same one
- nbr_slot: int32 [512, 2], P(('region', 'block')), may hold values from 0 to 15
- counts: int32 [32], P(('region', 'block')), may hold values from 8 to 16
Outputs:
- grad_obs: float32 [512, 32, 128], P(('region', 'block'))
- grad_tau: float32 [32], replicated
Inputs may be any that keep to these rules, and one draw needn't show every extreme that they name: `nbr_dev`: among the blocks of one device at most 4 name the same device. `nbr_slot`: column 0 is a slot on the in-region neighbour's device, column 1 a slot on the device of the previous region with the same index along block. `factor`: each block's matrix is the identity plus small entries.
All inputs are finite; a program needn't handle non-finite values.
Results may differ from a plain program's by a relative error of at most 0.0035.
Values may be sent and summed in bfloat16 or wider, within the bound.
A program may use at most 64 MiB of HBM per device.

v0:
```python
import jax
import jax.numpy as jnp
from jax import lax
from jax.sharding import PartitionSpec as P


def passed_along(value, axis, steps):
    count = lax.axis_size(axis)
    leading, last = (max(0, -steps), min(count, count - steps))
    return lax.ppermute(value, axis, [(source, source + steps) for source in range(leading, last)])


def shards(obs, predict, factor, tau, nbr_dev, nbr_slot, counts):
    nbd = obs.shape[0]
    chans = obs.shape[1]
    width = obs.shape[2]
    nblock = lax.axis_size("block")
    cap_size = max(2, 2 * nbd // nblock)
    total_slots = nblock * cap_size
    dest = nbr_dev[:, 0]
    slot_one = nbr_slot[:, 0]
    slot_two = nbr_slot[:, 1]
    onehot = (dest[:, None] == jnp.arange(nblock, dtype=jnp.int32)[None, :]).astype(jnp.int32)
    before = jnp.cumsum(onehot, axis=0) - onehot
    rank_in = jnp.sum(before * onehot, axis=1)
    flat = dest * cap_size + rank_in
    match = (flat[:, None] == jnp.arange(total_slots, dtype=jnp.int32)[None, :]).astype(jnp.int32)
    filled = jnp.sum(match, axis=0)
    req_flat = jnp.sum(match * slot_one[:, None], axis=0) + (1 - filled) * nbd
    request = req_flat.reshape(nblock, cap_size)
    region_all = lax.all_gather(obs, "block", axis=0, tiled=True)
    near = jnp.take(region_all, dest * nbd + slot_one, axis=0)
    previous = passed_along(obs, "region", 1)
    far = jnp.take(previous, slot_two, axis=0)
    p_zero = predict[:, 0]
    p_one = predict[:, 1]
    err = obs.astype(jnp.float32) - jnp.einsum(
        "bcj,bjk->bck", near, p_zero, preferred_element_type=jnp.float32
    )
    err = err - jnp.einsum("bcj,bjk->bck", far, p_one, preferred_element_type=jnp.float32)
    err = err.astype(jnp.bfloat16)
    white = jnp.einsum("bcj,bjk->bck", err, factor, preferred_element_type=jnp.float32)
    live = (jnp.arange(nbd, dtype=jnp.int32) < counts[0]).astype(jnp.float32)
    weighted = (live[:, None, None] * tau[None, :, None] * white).astype(jnp.bfloat16)
    adj = jnp.einsum("bck,bjk->bcj", weighted, factor, preferred_element_type=jnp.float32)
    adj16 = adj.astype(jnp.bfloat16)
    back_one = -jnp.einsum("bck,bjk->bcj", adj16, p_zero, preferred_element_type=jnp.float32)
    back_two = -jnp.einsum("bck,bjk->bcj", adj16, p_one, preferred_element_type=jnp.float32)
    placed = jnp.einsum(
        "bs,bcj->scj", match.astype(jnp.float32), back_one, precision=lax.Precision.HIGHEST
    )
    placed = placed.reshape(nblock, cap_size, chans, width)
    returned, owned_slots = (
        lax.all_to_all(placed, "block", split_axis=0, concat_axis=0, tiled=True),
        lax.all_to_all(request, "block", split_axis=0, concat_axis=0, tiled=True),
    )
    spread = (owned_slots.reshape(-1)[:, None] == jnp.arange(nbd, dtype=jnp.int32)[None, :]).astype(
        jnp.float32
    )
    add_one = jnp.einsum(
        "sb,scj->bcj",
        spread,
        returned.reshape(total_slots, chans, width),
        precision=lax.Precision.HIGHEST,
    )
    seam_hot = (slot_two[:, None] == jnp.arange(nbd, dtype=jnp.int32)[None, :]).astype(jnp.float32)
    seam_dense = jnp.einsum("bs,bcj->scj", seam_hot, back_two, precision=lax.Precision.HIGHEST)
    add_two = passed_along(seam_dense, "region", -1)
    grad_obs = adj + add_one + add_two
    squares = jnp.sum(live[:, None, None] * white * white, axis=(0, 2))
    live_count = jnp.sum(live)
    total_sq, total_live = lax.psum((squares, live_count), ("region", "block"))
    all_blocks = nbd * lax.axis_size("region") * nblock
    grad_tau = (0.5 * total_sq - 0.5 * width * total_live / tau) / (all_blocks * width)
    return (grad_obs, grad_tau)


def solution(mesh):
    in_specs = (
        P(("region", "block"), None, None),
        P(("region", "block"), None, None, None),
        P(("region", "block"), None, None),
        P(),
        P(("region", "block"), None),
        P(("region", "block"), None),
        P(("region", "block")),
    )
    out_specs = (P(("region", "block"), None, None), P())
    return jax.shard_map(shards, mesh=mesh, in_specs=in_specs, out_specs=out_specs, check_vma=False)
```

profile of v0, /device:TPU:0, one launch (start us, length us, event | category | flops | bytes accessed | tf_op | source)
XLA Modules:
  0.0 102.5 jit_solution(590737278167899570)
XLA Ops:
  7.2 0.0 copy-start
  7.2 0.0 copy-start.2
  7.2 0.0 copy-start.1
  7.2 0.0 all-gather.2.cloned.1.call-start
  7.2 0.7 all-gather.2.cloned.1.call-update
  7.9 0.2 copy-done.2
  8.1 4.8 %collective-permute-start = (bf16[16,32,128]{2,1,0:T(8,128)(2,1)S(1)}, bf16[16,32,128]{2,1,0:T(8,128)(2,1)S(1)}, u32[]{:S(2)}, u32[]{:S(2)}) collective-permute-start(bf16[16,32,128]{2,1,0:T(8,128)(2,1)S(1)} %copy-done.2), channel_id=1, source_target_pairs={{0,8},{8,16},{16,24},{1,9},{9,17},{17,25},{2,10},{10,18},{18,26},{... | collective-permute-start | bytes 393224 | tf_op jit(solution)/shard_map/ppermute | solution.py:10
  13.0 0.7 fusion.33
  13.8 0.8 select_reduce_fusion.1
  14.6 0.8 slice_bitcast_fusion.1
  15.4 0.1 convert_reduce_fusion
  15.5 0.7 add.50
  16.1 4.9 %all-to-all-start = ((s32[8,1,4]{2,1,0:T(1,128)}), s32[8,1,4]{2,1,0:T(1,128)S(1)}, u32[]{:S(2)}, u32[]{:S(2)}) async-start(s32[8,1,4]{2,1,0:T(1,128)} %bitcast.11), calls=%async_computation | async-start | bytes 8192 | tf_op jit(solution)/shard_map/all_to_all | solution.py:55
  21.7 0.8 and_bitcast_fusion.1
  22.4 0.7 broadcast_multiply_fusion
  23.2 0.0 collective-permute-done
  23.2 0.6 gather_fusion.1
  23.8 10.7 %all-gather.2.cloned.1.call-done = bf16[128,32,128]{2,1,0:T(8,128)(2,1)} async-done(((bf16[16,32,128]{2,1,0:T(8,128)(2,1)}), bf16[128,32,128]{2,1,0:T(8,128)(2,1)}) %all-gather.2.cloned.1.call-update) | async-done | bytes 1048592 | tf_op jit(solution)/shard_map/all_gather | solution.py:31
  34.5 1.8 %gather_fusion = bf16[16,32,128]{2,1,0:T(8,128)(2,1)S(1)} fusion(bf16[128,32,128]{2,1,0:T(8,128)(2,1)} %all-gather.2.cloned.1.call-done, s32[1024]{0:T(1024)S(1)} %pad_clamp_fusion.1), kind=kCustom, calls=%fused_computation | custom fusion | bytes 262208 | tf_op jit(solution)/shard_map/jit(_take)/gather | solution.py:32
  36.3 1.4 %convolution_subtract_fusion.1 = f32[16,32,128]{2,1,0:T(8,128)S(1)} fusion(bf16[16,2,128,128]{3,2,1,0:T(8,128)(2,1)} %param.8, bf16[16,32,128]{2,1,0:T(8,128)(2,1)S(1)} %copy-done.2, bf16[16,32,128]{2,1,0:T(8,128)(2,1)S(1)} %gather_fusion, pred[16]{0:T(512)(128)(4,1)S(1)} %get-tuple-element.6), kind=kOutput, calls=%fused_computation.5 | convolution fusion | flops 16973824 | bytes 1048592 | tf_op jit(solution)/shard_map/bcj,bjk->bck/dot_general | solution.py:37
  37.6 0.0 copy-done
  37.6 0.0 copy-done.1
  37.7 0.6 fusion.12
  38.2 0.4 fusion.18
  38.6 0.4 convolution_negate_fusion.1
  39.0 0.7 fusion.16
  39.8 0.9 copy.17
  40.7 0.0 all-to-all-done
  40.7 3.5 %all-to-all-start.1 = ((f32[8,4,32,128]{3,1,2,0:T(4,128)}), f32[8,4,32,128]{3,1,2,0:T(4,128)S(1)}, u32[]{:S(2)}, u32[]{:S(2)}) async-start(f32[8,4,32,128]{3,1,2,0:T(4,128)} %copy.17), calls=%async_computation.1 | async-start | bytes 1048576 | tf_op jit(solution)/shard_map/all_to_all | solution.py:54
  44.2 0.6 fusion.47
  44.8 0.5 broadcast.119
  45.3 0.7 reduce.3
  46.0 0.1 eq.68
  46.0 0.4 convolution_negate_fusion
  46.4 0.4 fusion.13
  46.8 0.1 copy.21
  46.9 1.3 %collective-permute-start.1 = (f32[16,32,128]{2,1,0:T(8,128)S(1)}, f32[16,32,128]{2,1,0:T(8,128)S(1)}, u32[]{:S(2)}, u32[]{:S(2)}) collective-permute-start(f32[16,32,128]{2,1,0:T(8,128)S(1)} %copy.21), channel_id=1, source_target_pairs={{8,0},{16,8},{24,16},{9,1},{17,9},{25,17},{10,2},{18,10},{26,18},{... | collective-permute-start | bytes 786440 | tf_op jit(solution)/shard_map/ppermute | solution.py:10
  48.2 44.3 %all-reduce = (f32[32]{0:T(128)S(1)}, f32[]{:T(128)}) all-reduce(f32[32]{0:T(128)S(1)} %get-tuple-element.12, f32[]{:T(128)} %fusion.47), channel_id=1, replica_groups=mesh['region'=4,'block'=8] {'region','block'}, use_global_device_ids=true, to_apply=%region_5.6 | all-reduce | flops 33 | bytes 264 | tf_op jit(solution)/shard_map/psum | solution.py:72
  93.1 0.0 copy-start.3
  93.2 0.6 copy-done.3
  93.8 0.5 fusion.43
  94.3 0.0 all-to-all-done.1
  94.3 0.1 copy.18
  94.5 0.3 fusion.35
  94.8 0.0 collective-permute-done.1
  94.8 0.9 fusion.15
  (5 shorter events, 0.1 us)
Async XLA Ops:
  7.2 30.5 %copy-start = (bf16[16,128,128]{2,1,0:T(8,128)(2,1)S(1)}, bf16[16,128,128]{2,1,0:T(8,128)(2,1)}, u32[]{:S(2)}) copy-start(bf16[16,128,128]{2,1,0:T(8,128)(2,1)} %param.9) | copy-start | bytes 1572868
  7.2 1.0 copy-start.2
  7.2 30.5 %copy-start.1 = (bf16[16,2,128,128]{3,2,1,0:T(8,128)(2,1)S(1)}, bf16[16,2,128,128]{3,2,1,0:T(8,128)(2,1)}, u32[]{:S(2)}) copy-start(bf16[16,2,128,128]{3,2,1,0:T(8,128)(2,1)} %param.8) | copy-start | bytes 3145732
  7.2 27.3 %all-gather.2.cloned.1.call-start = ((), (), s32[]{:S(2)}) async-start(), calls=%async_computation.2 | async-start | bytes 1179648 | tf_op jit(solution)/shard_map/all_gather | solution.py:31
  8.1 15.0 %collective-permute-start = (bf16[16,32,128]{2,1,0:T(8,128)(2,1)S(1)}, bf16[16,32,128]{2,1,0:T(8,128)(2,1)S(1)}, u32[]{:S(2)}, u32[]{:S(2)}) collective-permute-start(bf16[16,32,128]{2,1,0:T(8,128)(2,1)S(1)} %copy-done.2), channel_id=1, source_target_pairs={{0,8},{8,16},{16,24},{1,9},{9,17},{17,25},{2,10},{10,18},{18,26},{... | collective-permute-start | bytes 393224 | tf_op jit(solution)/shard_map/ppermute | solution.py:10
  16.1 24.5 %all-to-all-start = ((s32[8,1,4]{2,1,0:T(1,128)}), s32[8,1,4]{2,1,0:T(1,128)S(1)}, u32[]{:S(2)}, u32[]{:S(2)}) async-start(s32[8,1,4]{2,1,0:T(1,128)} %bitcast.11), calls=%async_computation | async-start | bytes 8192 | tf_op jit(solution)/shard_map/all_to_all | solution.py:55
  40.7 53.7 %all-to-all-start.1 = ((f32[8,4,32,128]{3,1,2,0:T(4,128)}), f32[8,4,32,128]{3,1,2,0:T(4,128)S(1)}, u32[]{:S(2)}, u32[]{:S(2)}) async-start(f32[8,4,32,128]{3,1,2,0:T(4,128)} %copy.17), calls=%async_computation.1 | async-start | bytes 1048576 | tf_op jit(solution)/shard_map/all_to_all | solution.py:54
  46.9 47.9 %collective-permute-start.1 = (f32[16,32,128]{2,1,0:T(8,128)S(1)}, f32[16,32,128]{2,1,0:T(8,128)S(1)}, u32[]{:S(2)}, u32[]{:S(2)}) collective-permute-start(f32[16,32,128]{2,1,0:T(8,128)S(1)} %copy.21), channel_id=1, source_target_pairs={{8,0},{16,8},{24,16},{9,1},{17,9},{25,17},{10,2},{18,10},{26,18},{... | collective-permute-start | bytes 786440 | tf_op jit(solution)/shard_map/ppermute | solution.py:10
  93.1 0.7 copy-start.3
Sparse Core Ops, SparseCore 0:
  9.6 24.7 all-gather.1
where the time goes:
time: 103 us
  blocking collectives  44.3 us (43%)
  between operations  15.5 us (15%)
  starting transfers between devices  14.5 us (14%)
  waiting for transfers between devices  11.4 us (11%)
  other arithmetic  6.61 us (6%)
  local copies, waits for them, and re-layouts  5.62 us (5%)
  matrix products  4.57 us (4%)
    psum x1, blocking collectives, shards(): total_sq, total_live = lax.psum((squares, live_count), ('region', 'block'))  44.3 us
    all_gather x1, waiting for transfers between devices, shards(): region_all = lax.all_gather(obs, 'block', axis=0, tiled=True)  10.7 us
    ppermute x2, starting transfers between devices, passed_along(): lax.ppermute(value, axis, [(source, source + steps) for source in range(l...  6.13 us
    all_to_all x1, starting transfers between devices, shards(): lax.all_to_all(request, 'block', split_axis=0, concat_axis=0, tiled=True)  4.88 us
    all_to_all x1, starting transfers between devices, shards(): lax.all_to_all(placed, 'block', split_axis=0, concat_axis=0, tiled=True)  3.49 us
  transfers between devices with their start and end apart: 5, of which 1 were waited for; matrix products, arithmetic and copies ran while one was open for 15% of the time, Pallas kernels for 0%

commit v1 on v0

v1 whole, which is shorter than its diff:
```python
import functools

import jax
import jax.numpy as jnp
from jax import lax
from jax.experimental import pallas as pl
from jax.experimental.pallas import tpu as pltpu
from jax.sharding import PartitionSpec as P

MESH = pl.DeviceIdType.MESH
LANES = 128


def kernel(
    nblock,
    nregion,
    cap,
    dev_ref,
    slot_ref,
    counts_ref,
    tau_ref,
    obs_hbm,
    predict_hbm,
    factor_hbm,
    out_ref,
    gtau_ref,
    obs,
    predict,
    factor,
    req_send,
    req_recv,
    near_send,
    near_recv,
    ret_send,
    ret_recv,
    seam_obs,
    seam_tgt,
    seam_tgt_in,
    seam_ret,
    seam_ret_in,
    place,
    spread,
    partial,
    back,
    adjoint,
    sq_send,
    sq_recv,
    rg_send,
    rg_recv,
    local_sem,
    req_ss,
    req_rs,
    near_ss,
    near_rs,
    ret_ss,
    ret_rs,
    sq_ss,
    sq_rs,
    rg_ss,
    rg_rs,
    seam_ss,
    seam_rs,
):
    nbd, chans, width = obs.shape
    rows = nbd * chans
    part = cap * chans
    lanes = req_send.shape[2]
    me = lax.axis_index("block")
    region = lax.axis_index("region")
    bf16, f32, i32 = jnp.bfloat16, jnp.float32, jnp.int32

    def each_peer(body):
        if nblock <= 8:
            for step in range(1, nblock):
                body(lax.rem(me + step, nblock))
        else:

            def run(step, carry):
                body(lax.rem(me + step, nblock))
                return carry

            lax.fori_loop(1, nblock, run, 0)

    def each_region(body):
        for step in range(1, nregion):
            body(lax.rem(region + step, nregion))

    def to_block(src, dst, ss, rs, peer):
        return pltpu.make_async_remote_copy(
            src_ref=src,
            dst_ref=dst,
            send_sem=ss,
            recv_sem=rs,
            device_id={"block": peer},
            device_id_type=MESH,
        )

    def to_region(src, dst, ss, rs, peer):
        return pltpu.make_async_remote_copy(
            src_ref=src,
            dst_ref=dst,
            send_sem=ss,
            recv_sem=rs,
            device_id={"region": peer},
            device_id_type=MESH,
        )

    barrier = pltpu.get_barrier_semaphore()
    each_peer(
        lambda peer: pl.semaphore_signal(
            barrier, inc=1, device_id={"block": peer}, device_id_type=MESH
        )
    )
    each_region(
        lambda peer: pl.semaphore_signal(
            barrier, inc=1, device_id={"region": peer}, device_id_type=MESH
        )
    )
    load_obs = pltpu.make_async_copy(obs_hbm, obs, local_sem.at[0])
    load_predict = pltpu.make_async_copy(predict_hbm, predict, local_sem.at[1])
    load_factor = pltpu.make_async_copy(factor_hbm, factor, local_sem.at[2])
    load_obs.start()
    load_predict.start()
    load_factor.start()

    dest = [dev_ref[h, 0] for h in range(nbd)]
    flat = []
    for h in range(nbd):
        rank = jnp.int32(0)
        for g in range(h):
            rank = rank + (dest[g] == dest[h]).astype(i32)
        flat.append(dest[h] * cap + rank)

    lane = lax.broadcasted_iota(i32, (nblock, lanes), 1)
    spot = lax.broadcasted_iota(i32, (nblock, lanes), 0) * cap + lane // chans
    spot = jnp.where(lane < part, spot, -1)
    wanted = jnp.full((nblock, lanes), -1, i32)
    for h in range(nbd):
        wanted = jnp.where(spot == flat[h], slot_ref[h, 0] * chans + lane % chans, wanted)
    for d in range(nblock):
        req_send[d] = wanted[d : d + 1]

    block_lane = lax.broadcasted_iota(i32, (1, rows), 1)
    owner_of = block_lane // chans
    flat_row = jnp.zeros((1, rows), i32)
    seam_row = jnp.zeros((1, rows), i32)
    for h in range(nbd):
        flat_row = jnp.where(owner_of == h, flat[h], flat_row)
        seam_row = jnp.where(owner_of == h, slot_ref[h, 1], seam_row)
    flat_row = flat_row * chans + block_lane % chans
    seam_tgt[...] = seam_row * chans + block_lane % chans

    pl.semaphore_wait(barrier, nblock - 1 + nregion - 1)

    def request(peer, mine):
        return to_block(req_send.at[peer], req_recv.at[mine], req_ss.at[peer], req_rs.at[mine], peer)

    each_peer(lambda peer: request(peer, me).start())
    req_recv[me] = req_send[me]

    down = lax.rem(region + 1, nregion)
    up = lax.rem(region + nregion - 1, nregion)
    seam_fwd = to_region(obs_hbm, seam_obs, seam_ss.at[0], seam_rs.at[0], down)
    seam_where = to_region(seam_tgt, seam_tgt_in, seam_ss.at[1], seam_rs.at[1], up)
    seam_bwd = to_region(seam_ret, seam_ret_in, seam_ss.at[2], seam_rs.at[2], up)
    has_prev = region > 0
    has_next = region < nregion - 1

    @pl.when(has_next)
    def _():
        seam_fwd.start()

    @pl.when(has_prev)
    def _():
        seam_where.start()

    load_obs.wait()
    pick_lane = lax.broadcasted_iota(i32, (part, rows), 1)

    def picked(peer):
        row = jnp.broadcast_to(req_recv[peer], (LANES, lanes))
        column = jnp.transpose(row)[:part]
        column = jnp.concatenate([column] * (rows // LANES), axis=1)
        mask = jnp.where(column == pick_lane, 1.0, 0.0).astype(bf16)
        got = jnp.dot(mask, obs[...].reshape(rows, width), preferred_element_type=f32)
        return got.astype(bf16).reshape(cap, chans, width)

    def span(d):
        return pl.ds(d * cap, cap)

    def serve(peer, mine):
        return to_block(
            near_send.at[span(peer)],
            near_recv.at[span(mine)],
            near_ss.at[peer],
            near_rs.at[mine],
            peer,
        )

    def answer(peer):
        request(me, peer).wait_recv()
        near_send[span(peer)] = picked(peer)
        serve(peer, me).start()

    each_peer(answer)
    near_recv[span(me)] = picked(me)

    place_row = lax.broadcasted_iota(i32, (part, rows), 0)

    def build(d):
        place[d] = jnp.where(flat_row - d * part == place_row, 1.0, 0.0).astype(bf16)
        spread[d] = jnp.where(
            req_recv[d][:, :part] == lax.broadcasted_iota(i32, (rows, part), 0), 1.0, 0.0
        ).astype(bf16)

    each_peer(build)
    build(me)

    @pl.when(has_prev)
    def _():
        seam_fwd.wait_recv()

    @pl.when(jnp.logical_not(has_prev))
    def _():
        seam_obs[...] = jnp.zeros_like(seam_obs)

    load_predict.wait()
    for g in range(nbd):
        partial[g] = obs[g].astype(f32) - jnp.dot(
            seam_obs[slot_ref[g, 1]], predict[g, 1], preferred_element_type=f32
        )
    load_factor.wait()

    eye = lax.broadcasted_iota(i32, (chans, LANES), 0) == lax.broadcasted_iota(
        i32, (chans, LANES), 1
    )
    tau_row = jnp.concatenate([tau_ref[...], jnp.zeros((1, LANES - chans), f32)], axis=1)
    tau_col = jnp.sum(jnp.where(eye, tau_row, 0.0), axis=1, keepdims=True)
    count = counts_ref[0]

    each_peer(lambda peer: serve(me, peer).wait_recv())

    squares = jnp.zeros((chans, width), f32)
    nt = (((1,), (1,)), ((), ()))
    for g in range(nbd):
        err = partial[g] - jnp.dot(near_recv[flat[g]], predict[g, 0], preferred_element_type=f32)
        white = jnp.dot(err.astype(bf16), factor[g], preferred_element_type=f32)
        live = (g < count).astype(f32)
        squares = squares + live * white * white
        weighted = (live * tau_col * white).astype(bf16)
        adj = lax.dot_general(weighted, factor[g], nt, preferred_element_type=f32)
        out_ref[g] = adj
        adj16 = adj.astype(bf16)
        adjoint[g] = adj16
        back[g] = lax.dot_general(adj16, predict[g, 0], nt, preferred_element_type=f32).astype(bf16)

    def placed(peer):
        got = jnp.dot(place[peer], back[...].reshape(rows, width), preferred_element_type=f32)
        return got.astype(bf16)

    def give(peer, mine):
        return to_block(ret_send.at[peer], ret_recv.at[mine], ret_ss.at[peer], ret_rs.at[mine], peer)

    def give_back(peer):
        ret_send[peer] = placed(peer)
        give(peer, me).start()

    each_peer(give_back)
    ret_recv[me] = placed(me)

    @pl.when(has_prev)
    def _():
        for g in range(nbd):
            seam_ret[g] = lax.dot_general(
                adjoint[g], predict[g, 1], nt, preferred_element_type=f32
            ).astype(bf16)
        seam_bwd.start()

    live_lane = lax.broadcasted_iota(i32, (1, LANES), 1) == chans
    sums = jnp.sum(
        jnp.where(eye, jnp.sum(squares, axis=1, keepdims=True), 0.0), axis=0, keepdims=True
    )
    sums = sums + jnp.where(live_lane, jnp.minimum(count, nbd).astype(f32), 0.0)
    sq_send[...] = sums

    def share(peer, mine):
        return to_block(sq_send, sq_recv.at[mine], sq_ss.at[peer], sq_rs.at[mine], peer)

    each_peer(lambda peer: share(peer, me).start())
    sq_recv[me] = sums
    each_peer(lambda peer: share(me, peer).wait_recv())
    line = sq_recv[0]
    for d in range(1, nblock):
        line = line + sq_recv[d]
    rg_send[...] = line

    def share_region(peer, mine):
        return to_region(rg_send, rg_recv.at[mine], rg_ss.at[peer], rg_rs.at[mine], peer)

    each_region(lambda peer: share_region(peer, region).start())
    rg_recv[region] = line

    @pl.when(has_next)
    def _():
        seam_where_in = to_region(seam_tgt, seam_tgt_in, seam_ss.at[1], seam_rs.at[1], up)
        seam_where_in.wait_recv()
        mask = jnp.where(
            seam_tgt_in[...] == lax.broadcasted_iota(i32, (rows, rows), 0), 1.0, 0.0
        ).astype(bf16)
        seam_bwd.wait_recv()
        got = jnp.dot(mask, seam_ret_in[...].reshape(rows, width), preferred_element_type=f32)
        out_ref[...] = out_ref[...] - got.reshape(nbd, chans, width)

    def add(d):
        got = jnp.dot(spread[d], ret_recv[d], preferred_element_type=f32)
        out_ref[...] = out_ref[...] - got.reshape(nbd, chans, width)

    add(me)

    each_region(lambda peer: share_region(region, peer).wait_recv())
    total = rg_recv[0]
    for r in range(1, nregion):
        total = total + rg_recv[r]
    total_live = jnp.sum(jnp.where(live_lane, total, 0.0), axis=1, keepdims=True)
    blocks = nbd * nblock * nregion
    gtau_ref[...] = (
        0.5 * total[:, :chans] - 0.5 * width * total_live / tau_ref[...]
    ) / (blocks * width)

    def take(peer):
        give(me, peer).wait_recv()
        add(peer)

    each_peer(take)

    def sent(peer):
        request(peer, me).wait_send()
        serve(peer, me).wait_send()
        give(peer, me).wait_send()
        share(peer, me).wait_send()

    each_peer(sent)
    each_region(lambda peer: share_region(peer, region).wait_send())

    @pl.when(has_next)
    def _():
        seam_fwd.wait_send()

    @pl.when(has_prev)
    def _():
        seam_where.wait_send()
        seam_bwd.wait_send()


def shards(obs, predict, factor, tau, nbr_dev, nbr_slot, counts):
    nbd, chans, width = obs.shape
    nblock = lax.axis_size("block")
    nregion = lax.axis_size("region")
    cap = max(2, 2 * nbd // nblock)
    rows = nbd * chans
    part = cap * chans
    lanes = -(-part // LANES) * LANES
    bf16, f32, i32 = jnp.bfloat16, jnp.float32, jnp.int32
    smem = pl.BlockSpec(memory_space=pltpu.SMEM)
    vmem = pl.BlockSpec(memory_space=pltpu.VMEM)
    hbm = pl.BlockSpec(memory_space=pl.ANY)
    dma = pltpu.SemaphoreType.DMA
    grad_obs, grad_tau = pl.pallas_call(
        functools.partial(kernel, nblock, nregion, cap),
        out_shape=(
            jax.ShapeDtypeStruct((nbd, chans, width), f32),
            jax.ShapeDtypeStruct((1, chans), f32),
        ),
        in_specs=[smem, smem, smem, vmem, hbm, hbm, hbm],
        out_specs=(vmem, vmem),
        scratch_shapes=[
            pltpu.VMEM((nbd, chans, width), bf16),
            pltpu.VMEM((nbd, 2, width, width), bf16),
            pltpu.VMEM((nbd, width, width), bf16),
            pltpu.VMEM((nblock, 1, lanes), i32),
            pltpu.VMEM((nblock, 1, lanes), i32),
            pltpu.VMEM((nblock * cap, chans, width), bf16),
            pltpu.VMEM((nblock * cap, chans, width), bf16),
            pltpu.VMEM((nblock, part, width), bf16),
            pltpu.VMEM((nblock, part, width), bf16),
            pltpu.VMEM((nbd, chans, width), bf16),
            pltpu.VMEM((1, rows), i32),
            pltpu.VMEM((1, rows), i32),
            pltpu.VMEM((nbd, chans, width), bf16),
            pltpu.VMEM((nbd, chans, width), bf16),
            pltpu.VMEM((nblock, part, rows), bf16),
            pltpu.VMEM((nblock, rows, part), bf16),
            pltpu.VMEM((nbd, chans, width), f32),
            pltpu.VMEM((nbd, chans, width), bf16),
            pltpu.VMEM((nbd, chans, width), bf16),
            pltpu.VMEM((1, LANES), f32),
            pltpu.VMEM((nblock, 1, LANES), f32),
            pltpu.VMEM((1, LANES), f32),
            pltpu.VMEM((nregion, 1, LANES), f32),
            dma((3,)),
            dma((nblock,)),
            dma((nblock,)),
            dma((nblock,)),
            dma((nblock,)),
            dma((nblock,)),
            dma((nblock,)),
            dma((nblock,)),
            dma((nblock,)),
            dma((nregion,)),
            dma((nregion,)),
            dma((3,)),
            dma((3,)),
        ],
        compiler_params=pltpu.CompilerParams(
            collective_id=0, has_side_effects=True, vmem_limit_bytes=40 << 20
        ),
        name="vecchia",
    )(nbr_dev, nbr_slot, counts, tau.reshape(1, chans), obs, predict, factor)
    return grad_obs, grad_tau.reshape(chans)


def solution(mesh):
    in_specs = (
        P(("region", "block"), None, None),
        P(("region", "block"), None, None, None),
        P(("region", "block"), None, None),
        P(),
        P(("region", "block"), None),
        P(("region", "block"), None),
        P(("region", "block")),
    )
    out_specs = (P(("region", "block"), None, None), P())
    return jax.shard_map(shards, mesh=mesh, in_specs=in_specs, out_specs=out_specs, check_vma=False)
```

time: 103 us -> 42.2 us (0.41)
  blocking collectives: 44.3 us -> 0 us
  Pallas kernels: 0 us -> 34.3 us
  starting transfers between devices: 14.5 us -> 0 us
  between operations: 15.5 us -> 1.3 us
  waiting for transfers between devices: 11.4 us -> 0 us
  other arithmetic: 6.61 us -> 0 us
  matrix products: 4.57 us -> 0 us
    psum x1 -> x0, blocking collectives: 44.3 us -> none  [shards(): total_sq, total_live = lax.psum((squares, live_count), ('region', 'block'))]
    pallas_call x0 -> x1, Pallas kernels: none -> 34.3 us  [shards(): pl.pallas_call(functools.partial(kernel, nblock, nregion, cap), out_shape...]
    all_gather x1 -> x0, waiting for transfers between devices: 10.7 us -> none  [shards(): region_all = lax.all_gather(obs, 'block', axis=0, tiled=True)]
    all_to_all x2 -> x0, starting transfers between devices: 8.37 us -> none  [the longest x1 4.88 us: shards(): lax.all_to_all(request, 'block', split_axis=0, concat_axis=0, tiled=True)]
    ppermute x2 -> x0, starting transfers between devices: 6.13 us -> none  [passed_along(): lax.ppermute(value, axis, [(source, source + steps) for source in range(l...]
    unnamed x8 -> x16, local copies, waits for them, and re-layouts: 0.87 us -> 6.37 us
    dot_general x8 -> x0, matrix products: 4.57 us -> none  [the longest x1 1.35 us: shards(): jnp.einsum('bcj,bjk->bck', near, p_zero, preferred_element_type=jnp.float32)]
    gather x2 -> x0, local copies, waits for them, and re-layouts: 2.37 us -> none  [the longest x1 1.8 us: shards(): near = jnp.take(region_all, dest * nbd + slot_one, axis=0)]
  transfers between devices with their start and end apart: 5 -> 0, of which waited for: 1 -> 0; matrix products, arithmetic and copies ran while one was open for 15% -> 0% of each run, Pallas kernels for 0% -> 0%
where the time goes in v1:
time: 42.2 us; the launch traced here: 42 us
  Pallas kernels  34.3 us (81%)
  local copies, waits for them, and re-layouts  6.37 us (15%)
  between operations  1.3 us (3%)
    pallas_call x1, Pallas kernels, shards(): pl.pallas_call(functools.partial(kernel, nblock, nregion, cap), out_shape...  34.3 us
    unnamed x16, local copies, waits for them, and re-layouts  6.37 us

profile of v1, /device:TPU:0, one launch (start us, length us, event | category | flops | bytes accessed | tf_op | source)
XLA Modules:
  0.0 42.0 jit_solution(15840211825802757283)
XLA Ops:
  1.3 0.0 copy-start.5
  1.3 0.6 %copy-done.5 = s32[16,1]{0,1:T(1,128)S(1)} copy-done((s32[16,1]{0,1:T(1,128)S(1)}, s32[16,1]{0,1:T(1,128)}, u32[]{:S(2)}) %copy-start.5) | copy-done | bytes 88
  1.9 0.0 copy-start.4
  1.9 0.1 copy.9.dev_ref
  2.0 0.6 %copy-done.4 = s32[16,2]{0,1:T(2,128)S(1)} copy-done((s32[16,2]{0,1:T(2,128)S(1)}, s32[16,2]{0,1:T(2,128)}, u32[]{:S(2)}) %copy-start.4) | copy-done | bytes 152
  2.6 0.0 copy-start.3
  2.6 0.1 copy.10.slot_ref
  2.7 0.6 %copy-done.3 = f32[32]{0:T(128)S(1)} copy-done((f32[32]{0:T(128)S(1)}, f32[32]{0:T(128)}, u32[]{:S(2)}) %copy-start.3) | copy-done | bytes 152
  3.3 0.0 copy-start
  3.3 1.2 %copy-done = bf16[16,2,128,128]{3,2,1,0:T(8,128)(2,1)S(1)} copy-done((bf16[16,2,128,128]{3,2,1,0:T(8,128)(2,1)S(1)}, bf16[16,2,128,128]{3,2,1,0:T(8,128)(2,1)}, u32[]{:S(2)}) %copy-start) | copy-done | bytes 1048600
  4.5 0.0 copy-start.1
  4.5 1.0 %copy-done.1 = bf16[16,128,128]{2,1,0:T(8,128)(2,1)S(1)} copy-done((bf16[16,128,128]{2,1,0:T(8,128)(2,1)S(1)}, bf16[16,128,128]{2,1,0:T(8,128)(2,1)}, u32[]{:S(2)}) %copy-start.1) | copy-done | bytes 524312
  5.5 0.0 copy-start.2
  5.5 0.9 %copy-done.2 = bf16[16,32,128]{2,1,0:T(8,128)(2,1)S(1)} copy-done((bf16[16,32,128]{2,1,0:T(8,128)(2,1)S(1)}, bf16[16,32,128]{2,1,0:T(8,128)(2,1)}, u32[]{:S(2)}) %copy-start.2) | copy-done | bytes 131096
  6.4 34.3 %vecchia.1 = (f32[16,32,128]{2,1,0:T(8,128)S(1)}, f32[1,32]{1,0:T(1,128)S(1)}) custom-call(s32[16,1]{1,0:T(8,128)S(1)} %copy.9.dev_ref, s32[16,2]{1,0:T(8,128)S(1)} %copy.10.slot_ref, s32[1]{0:T(128)S(6)} %copy.13.counts_ref, f32[1,32]{1,0:T(1,128)S(1)} %bitcast.2, bf16[16,32,128]{2,1,0:T(8,128)(2,1)S(1)} %copy-done.2, ...), custom_call_target="tpu_custom_call" | custom-call | tf_op jit(solution)/shard_map/vecchia/pallas_call | solution.py:368
  40.8 0.7 %copy.14 = f32[16,32,128]{2,1,0:T(8,128)} copy(f32[16,32,128]{2,1,0:T(8,128)S(1)} %get-tuple-element.8) | data formatting | bytes 524288
  41.5 0.5 %copy.15 = f32[32]{0:T(128)} copy(f32[32]{0:T(128)S(1)} %bitcast.3) | data formatting | bytes 256
Async XLA Ops:
  1.3 0.7 %copy-start.5 = (s32[16,1]{0,1:T(1,128)S(1)}, s32[16,1]{0,1:T(1,128)}, u32[]{:S(2)}) copy-start(s32[16,1]{0,1:T(1,128)} %param.11) | copy-start | bytes 196
  1.9 0.7 %copy-start.4 = (s32[16,2]{0,1:T(2,128)S(1)}, s32[16,2]{0,1:T(2,128)}, u32[]{:S(2)}) copy-start(s32[16,2]{0,1:T(2,128)} %param.12) | copy-start | bytes 388
  2.6 0.7 %copy-start.3 = (f32[32]{0:T(128)S(1)}, f32[32]{0:T(128)}, u32[]{:S(2)}) copy-start(f32[32]{0:T(128)} %param.10) | copy-start | bytes 388
  3.3 1.2 %copy-start = (bf16[16,2,128,128]{3,2,1,0:T(8,128)(2,1)S(1)}, bf16[16,2,128,128]{3,2,1,0:T(8,128)(2,1)}, u32[]{:S(2)}) copy-start(bf16[16,2,128,128]{3,2,1,0:T(8,128)(2,1)} %predict_hbm.1) | copy-start | bytes 3145732
  4.5 1.0 %copy-start.1 = (bf16[16,128,128]{2,1,0:T(8,128)(2,1)S(1)}, bf16[16,128,128]{2,1,0:T(8,128)(2,1)}, u32[]{:S(2)}) copy-start(bf16[16,128,128]{2,1,0:T(8,128)(2,1)} %factor_hbm.1) | copy-start | bytes 1572868
  5.5 0.9 %copy-start.2 = (bf16[16,32,128]{2,1,0:T(8,128)(2,1)S(1)}, bf16[16,32,128]{2,1,0:T(8,128)(2,1)}, u32[]{:S(2)}) copy-start(bf16[16,32,128]{2,1,0:T(8,128)(2,1)} %obs_hbm.1) | copy-start | bytes 393220

commit v2 on v1

--- a/solution.py
+++ b/solution.py
@@ -15,15 +15,19 @@
     nblock,
     nregion,
     cap,
-    dev_ref,
-    slot_ref,
-    counts_ref,
-    tau_ref,
+    dev_hbm,
+    slot_hbm,
+    counts_hbm,
+    tau_hbm,
     obs_hbm,
     predict_hbm,
     factor_hbm,
     out_ref,
     gtau_ref,
+    dev_ref,
+    slot_ref,
+    counts_ref,
+    tau_ref,
     obs,
     predict,
     factor,
@@ -105,6 +109,15 @@
             device_id_type=MESH,
         )
 
+    small = [
+        pltpu.make_async_copy(src, dst, local_sem.at[3 + i])
+        for i, (src, dst) in enumerate(
+            [(dev_hbm, dev_ref), (slot_hbm, slot_ref), (counts_hbm, counts_ref), (tau_hbm, tau_ref)]
+        )
+    ]
+    for copy in small:
+        copy.start()
+
     barrier = pltpu.get_barrier_semaphore()
     each_peer(
         lambda peer: pl.semaphore_signal(
@@ -123,7 +136,10 @@
     load_predict.start()
     load_factor.start()
 
-    dest = [dev_ref[h, 0] for h in range(nbd)]
+    for copy in small:
+        copy.wait()
+
+    dest = [dev_ref[0, h] for h in range(nbd)]
     flat = []
     for h in range(nbd):
         rank = jnp.int32(0)
@@ -136,7 +152,7 @@
     spot = jnp.where(lane < part, spot, -1)
     wanted = jnp.full((nblock, lanes), -1, i32)
     for h in range(nbd):
-        wanted = jnp.where(spot == flat[h], slot_ref[h, 0] * chans + lane % chans, wanted)
+        wanted = jnp.where(spot == flat[h], slot_ref[0, h] * chans + lane % chans, wanted)
     for d in range(nblock):
         req_send[d] = wanted[d : d + 1]
 
@@ -146,7 +162,7 @@
     seam_row = jnp.zeros((1, rows), i32)
     for h in range(nbd):
         flat_row = jnp.where(owner_of == h, flat[h], flat_row)
-        seam_row = jnp.where(owner_of == h, slot_ref[h, 1], seam_row)
+        seam_row = jnp.where(owner_of == h, slot_ref[1, h], seam_row)
     flat_row = flat_row * chans + block_lane % chans
     seam_tgt[...] = seam_row * chans + block_lane % chans
 
@@ -227,7 +243,7 @@
     load_predict.wait()
     for g in range(nbd):
         partial[g] = obs[g].astype(f32) - jnp.dot(
-            seam_obs[slot_ref[g, 1]], predict[g, 1], preferred_element_type=f32
+            seam_obs[slot_ref[1, g]], predict[g, 1], preferred_element_type=f32
         )
     load_factor.wait()
 
@@ -240,41 +256,25 @@
 
     each_peer(lambda peer: serve(me, peer).wait_recv())
 
-    squares = jnp.zeros((chans, width), f32)
     nt = (((1,), (1,)), ((), ()))
-    for g in range(nbd):
-        err = partial[g] - jnp.dot(near_recv[flat[g]], predict[g, 0], preferred_element_type=f32)
-        white = jnp.dot(err.astype(bf16), factor[g], preferred_element_type=f32)
-        live = (g < count).astype(f32)
-        squares = squares + live * white * white
-        weighted = (live * tau_col * white).astype(bf16)
-        adj = lax.dot_general(weighted, factor[g], nt, preferred_element_type=f32)
-        out_ref[g] = adj
-        adj16 = adj.astype(bf16)
-        adjoint[g] = adj16
-        back[g] = lax.dot_general(adj16, predict[g, 0], nt, preferred_element_type=f32).astype(bf16)
-
-    def placed(peer):
-        got = jnp.dot(place[peer], back[...].reshape(rows, width), preferred_element_type=f32)
-        return got.astype(bf16)
-
-    def give(peer, mine):
-        return to_block(ret_send.at[peer], ret_recv.at[mine], ret_ss.at[peer], ret_rs.at[mine], peer)
-
-    def give_back(peer):
-        ret_send[peer] = placed(peer)
-        give(peer, me).start()
-
-    each_peer(give_back)
-    ret_recv[me] = placed(me)
-
-    @pl.when(has_prev)
-    def _():
-        for g in range(nbd):
-            seam_ret[g] = lax.dot_general(
-                adjoint[g], predict[g, 1], nt, preferred_element_type=f32
-            ).astype(bf16)
-        seam_bwd.start()
+    every = range(nbd)
+    err = [
+        (
+            partial[g]
+            - jnp.dot(near_recv[flat[g]], predict[g, 0], preferred_element_type=f32)
+        ).astype(bf16)
+        for g in every
+    ]
+    white = [jnp.dot(err[g], factor[g], preferred_element_type=f32) for g in every]
+    live = [(g < count).astype(f32) for g in every]
+    weighted = [(live[g] * tau_col * white[g]).astype(bf16) for g in every]
+    squares = live[0] * white[0] * white[0]
+    for g in range(1, nbd):
+        squares = squares + live[g] * white[g] * white[g]
+    adj = [lax.dot_general(weighted[g], factor[g], nt, preferred_element_type=f32) for g in every]
+    for g in every:
+        out_ref[g] = adj[g]
+        adjoint[g] = adj[g].astype(bf16)
 
     live_lane = lax.broadcasted_iota(i32, (1, LANES), 1) == chans
     sums = jnp.sum(
@@ -288,6 +288,34 @@
 
     each_peer(lambda peer: share(peer, me).start())
     sq_recv[me] = sums
+
+    for g in every:
+        back[g] = lax.dot_general(
+            adjoint[g], predict[g, 0], nt, preferred_element_type=f32
+        ).astype(bf16)
+
+    def placed(peer):
+        got = jnp.dot(place[peer], back[...].reshape(rows, width), preferred_element_type=f32)
+        return got.astype(bf16)
+
+    def give(peer, mine):
+        return to_block(ret_send.at[peer], ret_recv.at[mine], ret_ss.at[peer], ret_rs.at[mine], peer)
+
+    def give_back(peer):
+        ret_send[peer] = placed(peer)
+        give(peer, me).start()
+
+    each_peer(give_back)
+    ret_recv[me] = placed(me)
+
+    @pl.when(has_prev)
+    def _():
+        for g in range(nbd):
+            seam_ret[g] = lax.dot_general(
+                adjoint[g], predict[g, 1], nt, preferred_element_type=f32
+            ).astype(bf16)
+        seam_bwd.start()
+
     each_peer(lambda peer: share(me, peer).wait_recv())
     line = sq_recv[0]
     for d in range(1, nblock):
@@ -361,9 +389,8 @@
     part = cap * chans
     lanes = -(-part // LANES) * LANES
     bf16, f32, i32 = jnp.bfloat16, jnp.float32, jnp.int32
-    smem = pl.BlockSpec(memory_space=pltpu.SMEM)
     vmem = pl.BlockSpec(memory_space=pltpu.VMEM)
-    hbm = pl.BlockSpec(memory_space=pl.ANY)
+    hbm = pl.BlockSpec(memory_space=pltpu.HBM)
     dma = pltpu.SemaphoreType.DMA
     grad_obs, grad_tau = pl.pallas_call(
         functools.partial(kernel, nblock, nregion, cap),
@@ -371,9 +398,13 @@
             jax.ShapeDtypeStruct((nbd, chans, width), f32),
             jax.ShapeDtypeStruct((1, chans), f32),
         ),
-        in_specs=[smem, smem, smem, vmem, hbm, hbm, hbm],
+        in_specs=[hbm] * 7,
         out_specs=(vmem, vmem),
         scratch_shapes=[
+            pltpu.SMEM((1, nbd), i32),
+            pltpu.SMEM((2, nbd), i32),
+            pltpu.SMEM((1,), i32),
+            pltpu.VMEM((1, chans), f32),
             pltpu.VMEM((nbd, chans, width), bf16),
             pltpu.VMEM((nbd, 2, width, width), bf16),
             pltpu.VMEM((nbd, width, width), bf16),
@@ -397,7 +428,7 @@
             pltpu.VMEM((nblock, 1, LANES), f32),
             pltpu.VMEM((1, LANES), f32),
             pltpu.VMEM((nregion, 1, LANES), f32),
-            dma((3,)),
+            dma((7,)),
             dma((nblock,)),
             dma((nblock,)),
             dma((nblock,)),
@@ -412,10 +443,10 @@
             dma((3,)),
         ],
         compiler_params=pltpu.CompilerParams(
-            collective_id=0, has_side_effects=True, vmem_limit_bytes=40 << 20
+            collective_id=0, has_side_effects=True
         ),
         name="vecchia",
-    )(nbr_dev, nbr_slot, counts, tau.reshape(1, chans), obs, predict, factor)
+    )(nbr_dev.T, nbr_slot.T, counts, tau.reshape(1, chans), obs, predict, factor)
     return grad_obs, grad_tau.reshape(chans)
 
 

time: 42.2 us -> 30.7 us (0.73)
  Pallas kernels: 34.3 us -> 27.1 us
  local copies, waits for them, and re-layouts: 6.37 us -> 2.19 us
    pallas_call x1, Pallas kernels: 34.3 us -> 27.1 us  [shards(): pl.pallas_call(functools.partial(kernel, nblock, nregion, cap), out_shape...]
    unnamed x16 -> x4, local copies, waits for them, and re-layouts: 6.37 us -> 2.19 us
where the time goes in v2:
time: 30.7 us; the launch traced here: 30.6 us
  Pallas kernels  27.1 us (88%)
  local copies, waits for them, and re-layouts  2.19 us (7%)
  between operations  1.3 us (4%)
    pallas_call x1, Pallas kernels, shards(): pl.pallas_call(functools.partial(kernel, nblock, nregion, cap), out_shape...  27.1 us
    unnamed x4, local copies, waits for them, and re-layouts  2.19 us

profile of v2, /device:TPU:0, one launch (start us, length us, event | category | flops | bytes accessed | tf_op | source)
XLA Modules:
  0.0 30.6 jit_solution(9880158721554518201)
XLA Ops:
  1.3 27.1 %vecchia.1 = (f32[16,32,128]{2,1,0:T(8,128)}, f32[1,32]{1,0:T(1,128)}) custom-call(s32[1,16]{1,0:T(1,128)} %bitcast.5, s32[2,16]{1,0:T(2,128)} %bitcast.4, s32[1]{0:T(128)S(6)} %copy.11.counts_hbm, f32[1,32]{1,0:T(1,128)} %bitcast.6, bf16[16,32,128]{2,1,0:T(8,128)(2,1)} %obs_hbm.1, bf16[16,2,128,128]{3,2,1,0:T(8,128)(2,1)} %predict_hbm.1, ...), custom_call_target="tpu_custom_call" | custom-call | tf_op jit(solution)/shard_map/vecchia/pallas_call | solution.py:395
  28.4 0.0 copy-start
  28.4 1.7 %copy.12 = f32[16,32,128]{2,1,0:T(8,128)} copy(f32[16,32,128]{2,1,0:T(8,128)} %get-tuple-element.8) | data formatting | bytes 524288
  30.1 0.0 copy-done
  30.1 0.5 %copy.13 = f32[32]{0:T(128)} copy(f32[32]{0:T(128)S(1)} %bitcast.7) | data formatting | bytes 256
Async XLA Ops:
  28.4 1.7 %copy-start = (f32[1,32]{1,0:T(1,128)S(1)}, f32[1,32]{1,0:T(1,128)}, u32[]{:S(2)}) copy-start(f32[1,32]{1,0:T(1,128)} %get-tuple-element.5) | copy-start | bytes 388

commit v3 on v2

--- a/solution.py
+++ b/solution.py
@@ -42,7 +42,8 @@
     seam_tgt_in,
     seam_ret,
     seam_ret_in,
-    place,
+    held,
+    held_ref,
     spread,
     partial,
     back,
@@ -69,21 +70,32 @@
     rows = nbd * chans
     part = cap * chans
     lanes = req_send.shape[2]
+    group = 2 if nblock % 2 == 0 and part % LANES == 0 else 1
     me = lax.axis_index("block")
     region = lax.axis_index("region")
     bf16, f32, i32 = jnp.bfloat16, jnp.float32, jnp.int32
 
-    def each_peer(body):
+    half = me // (nblock // 2)
+
+    def farthest(turn):
+        below = nblock - 1 - turn - (me + turn + 1) // nblock
+        above = turn + (turn - me + nblock) // nblock
+        return below + half * (above - below)
+
+    def each_peer(body, nearest=False):
+        def visit(turn):
+            body(farthest(nblock - 2 - turn if nearest else turn))
+
         if nblock <= 8:
-            for step in range(1, nblock):
-                body(lax.rem(me + step, nblock))
+            for turn in range(nblock - 1):
+                visit(turn)
         else:
 
-            def run(step, carry):
-                body(lax.rem(me + step, nblock))
+            def run(turn, carry):
+                visit(turn)
                 return carry
 
-            lax.fori_loop(1, nblock, run, 0)
+            lax.fori_loop(0, nblock - 1, run, 0)
 
     def each_region(body):
         for step in range(1, nregion):
@@ -158,13 +170,19 @@
 
     block_lane = lax.broadcasted_iota(i32, (1, rows), 1)
     owner_of = block_lane // chans
-    flat_row = jnp.zeros((1, rows), i32)
     seam_row = jnp.zeros((1, rows), i32)
     for h in range(nbd):
-        flat_row = jnp.where(owner_of == h, flat[h], flat_row)
         seam_row = jnp.where(owner_of == h, slot_ref[1, h], seam_row)
-    flat_row = flat_row * chans + block_lane % chans
     seam_tgt[...] = seam_row * chans + block_lane % chans
+
+    place_lane = lax.broadcasted_iota(i32, (1, LANES), 1)
+    holder = jnp.full((1, LANES), nbd, i32)
+    for h in range(nbd):
+        holder = jnp.where(place_lane == flat[h], h, holder)
+    held[...] = holder
+    load_held = pltpu.make_async_copy(held, held_ref, local_sem.at[7])
+    load_held.start()
+    back[nbd] = jnp.zeros((chans, width), bf16)
 
     pl.semaphore_wait(barrier, nblock - 1 + nregion - 1)
 
@@ -218,19 +236,20 @@
         near_send[span(peer)] = picked(peer)
         serve(peer, me).start()
 
-    each_peer(answer)
+    each_peer(answer, nearest=True)
     near_recv[span(me)] = picked(me)
 
-    place_row = lax.broadcasted_iota(i32, (part, rows), 0)
-
-    def build(d):
-        place[d] = jnp.where(flat_row - d * part == place_row, 1.0, 0.0).astype(bf16)
-        spread[d] = jnp.where(
-            req_recv[d][:, :part] == lax.broadcasted_iota(i32, (rows, part), 0), 1.0, 0.0
+    def build(chip):
+        wanted_row = jnp.concatenate(
+            [req_recv[chip * group + i][:, :part] for i in range(group)], axis=1
+        )
+        spread[chip] = jnp.where(
+            wanted_row == lax.broadcasted_iota(i32, (rows, group * part), 0), 1.0, 0.0
         ).astype(bf16)
 
-    each_peer(build)
-    build(me)
+    for chip in range(nblock // group):
+        build(chip)
+    load_held.wait()
 
     @pl.when(has_prev)
     def _():
@@ -271,11 +290,6 @@
     squares = live[0] * white[0] * white[0]
     for g in range(1, nbd):
         squares = squares + live[g] * white[g] * white[g]
-    adj = [lax.dot_general(weighted[g], factor[g], nt, preferred_element_type=f32) for g in every]
-    for g in every:
-        out_ref[g] = adj[g]
-        adjoint[g] = adj[g].astype(bf16)
-
     live_lane = lax.broadcasted_iota(i32, (1, LANES), 1) == chans
     sums = jnp.sum(
         jnp.where(eye, jnp.sum(squares, axis=1, keepdims=True), 0.0), axis=0, keepdims=True
@@ -289,24 +303,29 @@
     each_peer(lambda peer: share(peer, me).start())
     sq_recv[me] = sums
 
+    adj = [lax.dot_general(weighted[g], factor[g], nt, preferred_element_type=f32) for g in every]
+    for g in every:
+        out_ref[g] = adj[g]
+        adjoint[g] = adj[g].astype(bf16)
+
     for g in every:
         back[g] = lax.dot_general(
             adjoint[g], predict[g, 0], nt, preferred_element_type=f32
         ).astype(bf16)
 
-    def placed(peer):
-        got = jnp.dot(place[peer], back[...].reshape(rows, width), preferred_element_type=f32)
-        return got.astype(bf16)
+    def pack(dst, peer):
+        for k in range(cap):
+            dst[k * chans : (k + 1) * chans] = back[held_ref[0, peer * cap + k]]
 
     def give(peer, mine):
         return to_block(ret_send.at[peer], ret_recv.at[mine], ret_ss.at[peer], ret_rs.at[mine], peer)
 
     def give_back(peer):
-        ret_send[peer] = placed(peer)
+        pack(ret_send.at[peer], peer)
         give(peer, me).start()
 
     each_peer(give_back)
-    ret_recv[me] = placed(me)
+    pack(ret_recv.at[me], me)
 
     @pl.when(has_prev)
     def _():
@@ -316,7 +335,7 @@
             ).astype(bf16)
         seam_bwd.start()
 
-    each_peer(lambda peer: share(me, peer).wait_recv())
+    each_peer(lambda peer: share(me, peer).wait_recv(), nearest=True)
     line = sq_recv[0]
     for d in range(1, nblock):
         line = line + sq_recv[d]
@@ -339,11 +358,14 @@
         got = jnp.dot(mask, seam_ret_in[...].reshape(rows, width), preferred_element_type=f32)
         out_ref[...] = out_ref[...] - got.reshape(nbd, chans, width)
 
-    def add(d):
-        got = jnp.dot(spread[d], ret_recv[d], preferred_element_type=f32)
+    def add(chip):
+        blocks_back = ret_recv[pl.ds(chip * group, group)].reshape(group * part, width)
+        got = jnp.dot(spread[chip], blocks_back, preferred_element_type=f32)
         out_ref[...] = out_ref[...] - got.reshape(nbd, chans, width)
 
-    add(me)
+    each_peer(lambda peer: give(me, peer).wait_recv(), nearest=True)
+    for chip in range(nblock // group):
+        add(chip)
 
     each_region(lambda peer: share_region(region, peer).wait_recv())
     total = rg_recv[0]
@@ -355,12 +377,6 @@
         0.5 * total[:, :chans] - 0.5 * width * total_live / tau_ref[...]
     ) / (blocks * width)
 
-    def take(peer):
-        give(me, peer).wait_recv()
-        add(peer)
-
-    each_peer(take)
-
     def sent(peer):
         request(peer, me).wait_send()
         serve(peer, me).wait_send()
@@ -388,6 +404,7 @@
     rows = nbd * chans
     part = cap * chans
     lanes = -(-part // LANES) * LANES
+    group = 2 if nblock % 2 == 0 and part % LANES == 0 else 1
     bf16, f32, i32 = jnp.bfloat16, jnp.float32, jnp.int32
     vmem = pl.BlockSpec(memory_space=pltpu.VMEM)
     hbm = pl.BlockSpec(memory_space=pltpu.HBM)
@@ -419,16 +436,17 @@
             pltpu.VMEM((1, rows), i32),
             pltpu.VMEM((nbd, chans, width), bf16),
             pltpu.VMEM((nbd, chans, width), bf16),
-            pltpu.VMEM((nblock, part, rows), bf16),
-            pltpu.VMEM((nblock, rows, part), bf16),
+            pltpu.VMEM((1, LANES), i32),
+            pltpu.SMEM((1, LANES), i32),
+            pltpu.VMEM((nblock // group, rows, group * part), bf16),
             pltpu.VMEM((nbd, chans, width), f32),
-            pltpu.VMEM((nbd, chans, width), bf16),
+            pltpu.VMEM((nbd + 1, chans, width), bf16),
             pltpu.VMEM((nbd, chans, width), bf16),
             pltpu.VMEM((1, LANES), f32),
             pltpu.VMEM((nblock, 1, LANES), f32),
             pltpu.VMEM((1, LANES), f32),
             pltpu.VMEM((nregion, 1, LANES), f32),
-            dma((7,)),
+            dma((8,)),
             dma((nblock,)),
             dma((nblock,)),
             dma((nblock,)),

time: 30.7 us -> 29.1 us (0.948)
  Pallas kernels: 27.1 us -> 25.5 us
    pallas_call x1, Pallas kernels: 27.1 us -> 25.5 us  [shards(): pl.pallas_call(functools.partial(kernel, nblock, nregion, cap), out_shape...]
where the time goes in v3:
time: 29.1 us; the launch traced here: 28.9 us
  Pallas kernels  25.5 us (88%)
  local copies, waits for them, and re-layouts  2.19 us (8%)
  between operations  1.3 us (4%)
    pallas_call x1, Pallas kernels, shards(): pl.pallas_call(functools.partial(kernel, nblock, nregion, cap), out_shape...  25.5 us
    unnamed x4, local copies, waits for them, and re-layouts  2.19 us

profile of v3, /device:TPU:0, one launch (start us, length us, event | category | flops | bytes accessed | tf_op | source)
XLA Modules:
  0.0 28.9 jit_solution(13373525392077524738)
XLA Ops:
  1.3 25.5 %vecchia.1 = (f32[16,32,128]{2,1,0:T(8,128)}, f32[1,32]{1,0:T(1,128)}) custom-call(s32[1,16]{1,0:T(1,128)} %bitcast.5, s32[2,16]{1,0:T(2,128)} %bitcast.4, s32[1]{0:T(128)S(6)} %copy.11.counts_hbm, f32[1,32]{1,0:T(1,128)} %bitcast.6, bf16[16,32,128]{2,1,0:T(8,128)(2,1)} %obs_hbm.1, bf16[16,2,128,128]{3,2,1,0:T(8,128)(2,1)} %predict_hbm.1, ...), custom_call_target="tpu_custom_call" | custom-call | tf_op jit(solution)/shard_map/vecchia/pallas_call | solution.py:412
  26.8 0.0 copy-start
  26.8 1.7 %copy.12 = f32[16,32,128]{2,1,0:T(8,128)} copy(f32[16,32,128]{2,1,0:T(8,128)} %get-tuple-element.8) | data formatting | bytes 524288
  28.4 0.0 copy-done
  28.4 0.5 %copy.13 = f32[32]{0:T(128)} copy(f32[32]{0:T(128)S(1)} %bitcast.7) | data formatting | bytes 256
Async XLA Ops:
  26.8 1.7 %copy-start = (f32[1,32]{1,0:T(1,128)S(1)}, f32[1,32]{1,0:T(1,128)}, u32[]{:S(2)}) copy-start(f32[1,32]{1,0:T(1,128)} %get-tuple-element.5) | copy-start | bytes 388

commit v4 on v3

--- a/solution.py
+++ b/solution.py
@@ -65,6 +65,8 @@
     rg_rs,
     seam_ss,
     seam_rs,
+    far_ss,
+    far_rs,
 ):
     nbd, chans, width = obs.shape
     rows = nbd * chans
@@ -97,6 +99,15 @@
 
             lax.fori_loop(0, nblock - 1, run, 0)
 
+    chip, core = me // 2, lax.rem(me, 2)
+    across = nblock // 2 - 1 - chip
+    whole = nblock * cap
+    ends = nblock == 8
+    at_end = chip * across == 0
+
+    def far(peer):
+        return jnp.logical_and(at_end, peer // 2 == across)
+
     def each_region(body):
         for step in range(1, nregion):
             body(lax.rem(region + step, nregion))
@@ -121,6 +132,16 @@
             device_id_type=MESH,
         )
 
+    if ends:
+
+        @pl.when(jnp.logical_not(at_end))
+        def _():
+            near_recv[whole:] = jnp.zeros((2 * nbd, chans, width), bf16)
+
+        @pl.when(at_end)
+        def _():
+            near_recv[pl.ds(across * 2 * cap, 2 * cap)] = jnp.zeros((2 * cap, chans, width), bf16)
+
     small = [
         pltpu.make_async_copy(src, dst, local_sem.at[3 + i])
         for i, (src, dst) in enumerate(
@@ -192,6 +213,19 @@
     each_peer(lambda peer: request(peer, me).start())
     req_recv[me] = req_send[me]
 
+    def far_slot(i):
+        return near_recv.at[pl.ds(whole + i * nbd, nbd)]
+
+    far_copy = to_block(obs_hbm, far_slot(core), far_ss.at[0], far_rs.at[0], across * 2 + core)
+    relay = to_block(
+        far_slot(core), far_slot(core), far_ss.at[1], far_rs.at[1], chip * 2 + 1 - core
+    )
+    if ends:
+
+        @pl.when(at_end)
+        def _():
+            far_copy.start()
+
     down = lax.rem(region + 1, nregion)
     up = lax.rem(region + nregion - 1, nregion)
     seam_fwd = to_region(obs_hbm, seam_obs, seam_ss.at[0], seam_rs.at[0], down)
@@ -231,24 +265,40 @@
             peer,
         )
 
+    def put(peer):
+        near_send[span(peer)] = picked(peer)
+        serve(peer, me).start()
+
+    def unless_far(peer, act):
+        if ends:
+            pl.when(jnp.logical_not(far(peer)))(act)
+        else:
+            act()
+
     def answer(peer):
         request(me, peer).wait_recv()
-        near_send[span(peer)] = picked(peer)
-        serve(peer, me).start()
+        unless_far(peer, lambda: put(peer))
 
     each_peer(answer, nearest=True)
     near_recv[span(me)] = picked(me)
-
-    def build(chip):
+    if ends:
+
+        @pl.when(at_end)
+        def _():
+            far_copy.wait_recv()
+            relay.start()
+
+
+    def build(pair):
         wanted_row = jnp.concatenate(
-            [req_recv[chip * group + i][:, :part] for i in range(group)], axis=1
-        )
-        spread[chip] = jnp.where(
+            [req_recv[pair * group + i][:, :part] for i in range(group)], axis=1
+        )
+        spread[pair] = jnp.where(
             wanted_row == lax.broadcasted_iota(i32, (rows, group * part), 0), 1.0, 0.0
         ).astype(bf16)
 
-    for chip in range(nblock // group):
-        build(chip)
+    for pair in range(nblock // group):
+        build(pair)
     load_held.wait()
 
     @pl.when(has_prev)
@@ -273,14 +323,26 @@
     tau_col = jnp.sum(jnp.where(eye, tau_row, 0.0), axis=1, keepdims=True)
     count = counts_ref[0]
 
-    each_peer(lambda peer: serve(me, peer).wait_recv())
+    source = flat
+    if ends:
+        at_far = [jnp.logical_and(at_end, dest[h] // 2 == across) for h in range(nbd)]
+        source = [
+            jnp.where(at_far[h], whole + lax.rem(dest[h], 2) * nbd + slot_ref[0, h], flat[h])
+            for h in range(nbd)
+        ]
+
+        @pl.when(at_end)
+        def _():
+            relay.wait_recv()
+
+    each_peer(lambda peer: unless_far(peer, lambda: serve(me, peer).wait_recv()), nearest=True)
 
     nt = (((1,), (1,)), ((), ()))
     every = range(nbd)
     err = [
         (
             partial[g]
-            - jnp.dot(near_recv[flat[g]], predict[g, 0], preferred_element_type=f32)
+            - jnp.dot(near_recv[source[g]], predict[g, 0], preferred_element_type=f32)
         ).astype(bf16)
         for g in every
     ]
@@ -358,14 +420,14 @@
         got = jnp.dot(mask, seam_ret_in[...].reshape(rows, width), preferred_element_type=f32)
         out_ref[...] = out_ref[...] - got.reshape(nbd, chans, width)
 
-    def add(chip):
-        blocks_back = ret_recv[pl.ds(chip * group, group)].reshape(group * part, width)
-        got = jnp.dot(spread[chip], blocks_back, preferred_element_type=f32)
+    def add(pair):
+        blocks_back = ret_recv[pl.ds(pair * group, group)].reshape(group * part, width)
+        got = jnp.dot(spread[pair], blocks_back, preferred_element_type=f32)
         out_ref[...] = out_ref[...] - got.reshape(nbd, chans, width)
 
     each_peer(lambda peer: give(me, peer).wait_recv(), nearest=True)
-    for chip in range(nblock // group):
-        add(chip)
+    for pair in range(nblock // group):
+        add(pair)
 
     each_region(lambda peer: share_region(region, peer).wait_recv())
     total = rg_recv[0]
@@ -379,11 +441,18 @@
 
     def sent(peer):
         request(peer, me).wait_send()
-        serve(peer, me).wait_send()
+        unless_far(peer, lambda: serve(peer, me).wait_send())
         give(peer, me).wait_send()
         share(peer, me).wait_send()
 
     each_peer(sent)
+    if ends:
+
+        @pl.when(at_end)
+        def _():
+            far_copy.wait_send()
+            relay.wait_send()
+
     each_region(lambda peer: share_region(peer, region).wait_send())
 
     @pl.when(has_next)
@@ -428,7 +497,7 @@
             pltpu.VMEM((nblock, 1, lanes), i32),
             pltpu.VMEM((nblock, 1, lanes), i32),
             pltpu.VMEM((nblock * cap, chans, width), bf16),
-            pltpu.VMEM((nblock * cap, chans, width), bf16),
+            pltpu.VMEM((nblock * cap + 2 * nbd, chans, width), bf16),
             pltpu.VMEM((nblock, part, width), bf16),
             pltpu.VMEM((nblock, part, width), bf16),
             pltpu.VMEM((nbd, chans, width), bf16),
@@ -459,6 +528,8 @@
             dma((nregion,)),
             dma((3,)),
             dma((3,)),
+            dma((2,)),
+            dma((2,)),
         ],
         compiler_params=pltpu.CompilerParams(
             collective_id=0, has_side_effects=True

time: 29.1 us -> 28.3 us (0.973)
  Pallas kernels: 25.5 us -> 24.6 us
    pallas_call x1, Pallas kernels: 25.5 us -> 24.6 us  [shards(): pl.pallas_call(functools.partial(kernel, nblock, nregion, cap), out_shape...]
where the time goes in v4:
time: 28.3 us; the launch traced here: 28.1 us
  Pallas kernels  24.6 us (87%)
  local copies, waits for them, and re-layouts  2.19 us (8%)
  between operations  1.3 us (5%)
    pallas_call x1, Pallas kernels, shards(): pl.pallas_call(functools.partial(kernel, nblock, nregion, cap), out_shape...  24.6 us
    unnamed x4, local copies, waits for them, and re-layouts  2.19 us

profile of v4, /device:TPU:0, one launch (start us, length us, event | category | flops | bytes accessed | tf_op | source)
XLA Modules:
  0.0 28.1 jit_solution(1807587550212128487)
XLA Ops:
  1.3 24.6 %vecchia.1 = (f32[16,32,128]{2,1,0:T(8,128)}, f32[1,32]{1,0:T(1,128)}) custom-call(s32[1,16]{1,0:T(1,128)} %bitcast.5, s32[2,16]{1,0:T(2,128)} %bitcast.4, s32[1]{0:T(128)S(6)} %copy.11.counts_hbm, f32[1,32]{1,0:T(1,128)} %bitcast.6, bf16[16,32,128]{2,1,0:T(8,128)(2,1)} %obs_hbm.1, bf16[16,2,128,128]{3,2,1,0:T(8,128)(2,1)} %predict_hbm.1, ...), custom_call_target="tpu_custom_call" | custom-call | tf_op jit(solution)/shard_map/vecchia/pallas_call | solution.py:481
  25.9 0.0 copy-start
  25.9 1.7 %copy.12 = f32[16,32,128]{2,1,0:T(8,128)} copy(f32[16,32,128]{2,1,0:T(8,128)} %get-tuple-element.8) | data formatting | bytes 524288
  27.6 0.0 copy-done
  27.6 0.5 %copy.13 = f32[32]{0:T(128)} copy(f32[32]{0:T(128)S(1)} %bitcast.7) | data formatting | bytes 256
Async XLA Ops:
  25.9 1.7 %copy-start = (f32[1,32]{1,0:T(1,128)S(1)}, f32[1,32]{1,0:T(1,128)}, u32[]{:S(2)}) copy-start(f32[1,32]{1,0:T(1,128)} %get-tuple-element.5) | copy-start | bytes 388

commit v5 on v4

--- a/solution.py
+++ b/solution.py
@@ -532,10 +532,15 @@
             dma((2,)),
         ],
         compiler_params=pltpu.CompilerParams(
-            collective_id=0, has_side_effects=True
+            collective_id=0, has_side_effects=True, vmem_limit_bytes=48 << 20
         ),
         name="vecchia",
-    )(nbr_dev.T, nbr_slot.T, counts, tau.reshape(1, chans), obs, predict, factor)
+    )(
+        *(
+            value if value is counts else pltpu.with_memory_space_constraint(value, pltpu.HBM)
+            for value in (nbr_dev.T, nbr_slot.T, counts, tau.reshape(1, chans), obs, predict, factor)
+        )
+    )
     return grad_obs, grad_tau.reshape(chans)
 
 

time: 28.3 us -> 26.6 us (0.940)
  local copies, waits for them, and re-layouts: 2.19 us -> 1.22 us
  Pallas kernels: 24.6 us -> 23.9 us
    unnamed x4 -> x2, local copies, waits for them, and re-layouts: 2.19 us -> 1.22 us
    pallas_call x1, Pallas kernels: 24.6 us -> 23.9 us  [shards(): pl.pallas_call(functools.partial(kernel, nblock, nregion, cap), out_shape...]
where the time goes in v5:
time: 26.6 us; the launch traced here: 26.4 us
  Pallas kernels  23.9 us (90%)
  between operations  1.29 us (5%)
  local copies, waits for them, and re-layouts  1.22 us (5%)
    pallas_call x1, Pallas kernels, shards(): pl.pallas_call(functools.partial(kernel, nblock, nregion, cap), out_shape...  23.9 us
    unnamed x2, local copies, waits for them, and re-layouts  1.22 us

profile of v5, /device:TPU:0, one launch (start us, length us, event | category | flops | bytes accessed | tf_op | source)
XLA Modules:
  0.0 26.4 jit_solution(12706610127376572206)
XLA Ops:
  1.3 23.9 %vecchia.1 = (f32[16,32,128]{2,1,0:T(8,128)S(1)}, f32[1,32]{1,0:T(1,128)S(1)}) custom-call(s32[1,16]{1,0:T(1,128)} %bitcast.6, s32[2,16]{1,0:T(2,128)} %bitcast.5, s32[1]{0:T(128)S(6)} %copy.11.counts_hbm, f32[1,32]{1,0:T(1,128)} %bitcast.7, bf16[16,32,128]{2,1,0:T(8,128)(2,1)} %obs_hbm.1, bf16[16,2,128,128]{3,2,1,0:T(8,128)(2,1)} %predict_hbm.1, ...), custom_call_target="tpu_custom_call" | custom-call | tf_op jit(solution)/shard_map/vecchia/pallas_call | solution.py:481
  25.2 0.7 %copy.12 = f32[16,32,128]{2,1,0:T(8,128)} copy(f32[16,32,128]{2,1,0:T(8,128)S(1)} %get-tuple-element.8) | data formatting | bytes 524288
  25.9 0.5 %copy.13 = f32[32]{0:T(128)} copy(f32[32]{0:T(128)S(1)} %bitcast.4) | data formatting | bytes 256
